TPU v7x, 32 devices: a whole 2x2x4 slice. The times are simulated.
32 devices in a mesh: seq: 2 (over y), fsdp: 16 (over z, x, core).
Axes of the slice: x: 2, y: 2, z: 4, core: 2. Of those that a mesh axis runs over, the one named last changes fastest.
Arguments:
- tokens: bfloat16 [16, 1024, 1024], P('fsdp', 'seq'), may hold values from -6 to 6
- blocks: int32 [16, 1024], P('fsdp'), may hold values from 0 to 7, never falling along the last dimension, each value on 1 to 256 neighbouring positions
- first_gain: bfloat16 [1024], P('fsdp'), may hold values from 0.5 to 1.5
- first_shift: bfloat16 [1024], P('fsdp'), may hold values from -1.5 to 1.5
- joint_weight: bfloat16 [1024, 3072], P('fsdp'), may hold values from -0.1875 to 0.1875
- joint_bias: bfloat16 [2, 1024], P(None, 'fsdp'), may hold values from -1.5 to 1.5
- output_weight: bfloat16 [1024, 1024], P('fsdp'), may hold values from -0.75 to 0.75
- output_bias: bfloat16 [1024], P('fsdp'), may hold values from -1.5 to 1.5
- second_gain: bfloat16 [1024], P('fsdp'), may hold values from 0.5 to 1.5
- second_shift: bfloat16 [1024], P('fsdp'), may hold values from -1.5 to 1.5
- upward_weight: bfloat16 [1024, 4096], P('fsdp'), may hold values from -0.1875 to 0.1875
- upward_bias: bfloat16 [4096], P('fsdp'), may hold values from -1.5 to 1.5
- downward_weight: bfloat16 [4096, 1024], P('fsdp'), may hold values from -0.125 to 0.125
- downward_bias: bfloat16 [1024], P('fsdp'), may hold values from -1.5 to 1.5
- cotangent: bfloat16 [16, 1024, 1024], P('fsdp', 'seq'), may hold values from -6 to 6
Outputs:
- result: bfloat16 [16, 1024, 1024], P('fsdp', 'seq')
- grad_tokens: float32 [16, 1024, 1024], P('fsdp', 'seq')
- grad_first_gain: float32 [1024], P('fsdp')
- grad_first_shift: float32 [1024], P('fsdp')
- grad_joint_weight: float32 [1024, 3072], P('fsdp')
- grad_joint_bias: float32 [2, 1024], P(None, 'fsdp')
- grad_output_weight: float32 [1024, 1024], P('fsdp')
- grad_output_bias: float32 [1024], P('fsdp')
- grad_second_gain: float32 [1024], P('fsdp')
- grad_second_shift: float32 [1024], P('fsdp')
- grad_upward_weight: float32 [1024, 4096], P('fsdp')
- grad_upward_bias: float32 [4096], P('fsdp')
- grad_downward_weight: float32 [4096, 1024], P('fsdp')
- grad_downward_bias: float32 [1024], P('fsdp')
Inputs may be any that keep to these rules, and one draw needn't show every extreme that they name: `blocks`: along each sequence the block number never falls; every block has 1 to 256 tokens, and one has exactly 256.
All inputs are finite; a program needn't handle non-finite values.
Results may differ from a plain program's by a relative error of at most 0.014.
Values may be sent and summed in bfloat16 or wider, within the bound.
No kernel may reach another device: no remote copies, remote signals or barrier semaphores. Data moves between devices by JAX's collectives and lax.ppermute only.
A program may use at most 192 MiB of HBM per device.

v0:
```python
import jax
import jax.numpy as jnp
from jax import lax
from jax.sharding import PartitionSpec as P

HEADS = 16
HEAD_DIM = 64
EPSILON = 1e-05


def scaled_norm(values, gain):
    center = values - jnp.mean(values, axis=-1, keepdims=True)
    spread = jnp.mean(center * center, axis=-1, keepdims=True)
    return center * lax.rsqrt(spread + EPSILON) * gain


def gelu_tanh(values):
    return jax.nn.gelu(values, approximate=True)


def matmul(left, right):
    return jnp.dot(left, right, preferred_element_type=jnp.float32)


def left_contract(left, right):
    return lax.dot_general(
        left, right, (((0,), (0,)), ((), ())), preferred_element_type=jnp.float32
    )


def right_contract(left, right):
    return lax.dot_general(
        left, right, (((1,), (1,)), ((), ())), preferred_element_type=jnp.float32
    )


def masked_scores(queries, keys_in, slope, distance, allowed):
    scores = right_contract(queries, keys_in) * HEAD_DIM ** (-0.5) - slope * distance
    return jnp.where(allowed, scores, -1e30)


def attend_heads(heads, slopes, distance, allowed):

    def one_head(packed):
        queries, keys_in, values_in, slope = packed
        scores = masked_scores(queries, keys_in, slope, distance, allowed)
        top_score = jnp.max(scores, axis=1, keepdims=True)
        totals = jnp.sum(jnp.exp(scores - top_score), axis=1, keepdims=True)
        log_total = top_score + jnp.log(totals)
        probs = jnp.exp(scores - log_total).astype(jnp.bfloat16)
        return (matmul(probs, values_in).astype(jnp.bfloat16), log_total[:, 0])

    return lax.map(one_head, (heads[0], heads[1], heads[2], slopes))


def attend_back(heads, log_totals, grad_heads, slopes, distance, allowed):

    def one_head(packed):
        queries, keys_in, values_in, log_total, grad_head, slope = packed
        scores = masked_scores(queries, keys_in, slope, distance, allowed)
        probs = jnp.exp(scores - log_total[:, None])
        grad_probs = right_contract(grad_head, values_in)
        inner = jnp.sum(probs * grad_probs, axis=1, keepdims=True)
        grad_scores = (probs * (grad_probs - inner)).astype(jnp.bfloat16)
        factor = HEAD_DIM ** (-0.5)
        grad_queries = matmul(grad_scores, keys_in) * factor
        grad_keys = left_contract(grad_scores, queries) * factor
        grad_values = left_contract(probs.astype(jnp.bfloat16), grad_head)
        return jnp.stack([grad_queries, grad_keys, grad_values]).astype(jnp.bfloat16)

    return lax.map(one_head, (heads[0], heads[1], heads[2], log_totals, grad_heads, slopes))


def per_device(
    tokens,
    blocks,
    first_gain,
    first_shift,
    joint_weight,
    joint_bias,
    output_weight,
    output_bias,
    second_gain,
    second_shift,
    upward_weight,
    upward_bias,
    downward_weight,
    downward_bias,
    cotangent,
):
    groups = lax.axis_size("seq")
    token_count = tokens.shape[1]
    model_width = tokens.shape[2]
    seq_length = token_count * groups
    local_heads = HEADS // groups
    group_width = model_width // groups
    inputs = tokens[0].astype(jnp.float32)
    attn_set = (
        lax.all_gather(first_gain, "fsdp", axis=0, tiled=True),
        lax.all_gather(first_shift, "fsdp", axis=0, tiled=True),
        lax.all_gather(joint_weight, "fsdp", axis=0, tiled=True),
        lax.all_gather(joint_bias, "fsdp", axis=1, tiled=True),
        lax.all_gather(output_weight, "fsdp", axis=0, tiled=True),
        lax.all_gather(output_bias, "fsdp", axis=0, tiled=True),
    )
    normed_one = (
        scaled_norm(inputs, attn_set[0].astype(jnp.float32)) + attn_set[1].astype(jnp.float32)
    ).astype(jnp.bfloat16)
    bias_full = jnp.concatenate(
        [attn_set[3][0], jnp.zeros((model_width,), jnp.bfloat16), attn_set[3][1]]
    ).astype(jnp.float32)
    joint = (matmul(normed_one, attn_set[2]) + bias_full).astype(jnp.bfloat16)
    joint = joint.reshape(token_count, 3, groups, group_width)
    heads = lax.all_to_all(joint, "seq", split_axis=2, concat_axis=0, tiled=True)
    heads = heads.reshape(seq_length, 3, local_heads, HEAD_DIM).transpose(1, 2, 0, 3)
    positions = jnp.arange(seq_length)
    distance = jnp.abs(positions[:, None] - positions[None, :]).astype(jnp.float32)
    block_row = blocks[0]
    allowed = block_row[None, :] <= block_row[:, None]
    head_index = lax.axis_index("seq") * local_heads + jnp.arange(local_heads)
    slopes = jnp.exp2(-8.0 * (head_index.astype(jnp.float32) + 1.0) / HEADS)
    attended, log_totals = attend_heads(heads, slopes, distance, allowed)
    flat_heads = attended.transpose(1, 0, 2).reshape(seq_length, 1, group_width)
    mixed = lax.all_to_all(flat_heads, "seq", split_axis=0, concat_axis=1, tiled=True).reshape(
        token_count, model_width
    )
    hidden = inputs + matmul(mixed, attn_set[4]) + attn_set[5].astype(jnp.float32)
    mlp_set = (
        lax.all_gather(second_gain, "fsdp", axis=0, tiled=True),
        lax.all_gather(second_shift, "fsdp", axis=0, tiled=True),
        lax.all_gather(upward_weight, "fsdp", axis=0, tiled=True),
        lax.all_gather(upward_bias, "fsdp", axis=0, tiled=True),
        lax.all_gather(downward_weight, "fsdp", axis=0, tiled=True),
        lax.all_gather(downward_bias, "fsdp", axis=0, tiled=True),
    )
    normed_two = (
        scaled_norm(hidden, mlp_set[0].astype(jnp.float32)) + mlp_set[1].astype(jnp.float32)
    ).astype(jnp.bfloat16)
    upward = matmul(normed_two, mlp_set[2]) + mlp_set[3].astype(jnp.float32)
    activated = gelu_tanh(upward).astype(jnp.bfloat16)
    output = hidden + matmul(activated, mlp_set[4]) + mlp_set[5].astype(jnp.float32)
    back_gain_two, back_upward, back_downward = (
        lax.all_gather(second_gain, "fsdp", axis=0, tiled=True),
        lax.all_gather(upward_weight, "fsdp", axis=0, tiled=True),
        lax.all_gather(downward_weight, "fsdp", axis=0, tiled=True),
    )
    grad_output = cotangent[0].astype(jnp.float32)
    grad_low = grad_output.astype(jnp.bfloat16)
    grad_down_bias = jnp.sum(grad_low.astype(jnp.float32), axis=0)
    grad_down_weight = left_contract(activated, grad_low)
    grad_act = right_contract(grad_low, back_downward)
    gelu_back = jax.vjp(gelu_tanh, upward)[1]
    grad_up = gelu_back(grad_act)[0].astype(jnp.bfloat16)
    grad_up_bias = jnp.sum(grad_up.astype(jnp.float32), axis=0)
    grad_up_weight = left_contract(normed_two, grad_up)
    grad_normed_two = right_contract(grad_up, back_upward)
    norm_two_back = jax.vjp(scaled_norm, hidden, back_gain_two.astype(jnp.float32))[1]
    grad_hidden_norm, grad_gain_two = norm_two_back(grad_normed_two)
    grad_shift_two = jnp.sum(grad_normed_two, axis=0)
    grad_hidden = grad_output + grad_hidden_norm
    back_gain_one, back_joint, back_output = (
        lax.all_gather(first_gain, "fsdp", axis=0, tiled=True),
        lax.all_gather(joint_weight, "fsdp", axis=0, tiled=True),
        lax.all_gather(output_weight, "fsdp", axis=0, tiled=True),
    )
    hidden_low = grad_hidden.astype(jnp.bfloat16)
    grad_out_bias = jnp.sum(hidden_low.astype(jnp.float32), axis=0)
    grad_out_weight = left_contract(mixed, hidden_low)
    grad_mixed = right_contract(hidden_low, back_output).astype(jnp.bfloat16)
    grad_mixed = grad_mixed.reshape(token_count, groups, group_width)
    grad_heads = lax.all_to_all(grad_mixed, "seq", split_axis=1, concat_axis=0, tiled=True)
    grad_heads = grad_heads.reshape(seq_length, local_heads, HEAD_DIM).transpose(1, 0, 2)
    grad_stack = attend_back(heads, log_totals, grad_heads, slopes, distance, allowed)
    grad_stack = grad_stack.transpose(2, 1, 0, 3).reshape(seq_length, 3, 1, group_width)
    grad_joint = lax.all_to_all(grad_stack, "seq", split_axis=0, concat_axis=2, tiled=True)
    grad_joint = grad_joint.reshape(token_count, 3 * model_width)
    joint_sums = jnp.sum(grad_joint.astype(jnp.float32), axis=0)
    grad_joint_bias = jnp.stack([joint_sums[:model_width], joint_sums[2 * model_width :]])
    grad_joint_weight = left_contract(normed_one, grad_joint)
    grad_normed_one = right_contract(grad_joint, back_joint)
    norm_one_back = jax.vjp(scaled_norm, inputs, back_gain_one.astype(jnp.float32))[1]
    grad_input_norm, grad_gain_one = norm_one_back(grad_normed_one)
    grad_shift_one = jnp.sum(grad_normed_one, axis=0)
    grad_inputs = grad_hidden + grad_input_norm
    every_sum = (
        lax.psum_scatter(grad_gain_one, "fsdp", scatter_dimension=0, tiled=True),
        lax.psum_scatter(grad_shift_one, "fsdp", scatter_dimension=0, tiled=True),
        lax.psum_scatter(grad_joint_weight, "fsdp", scatter_dimension=0, tiled=True),
        lax.psum_scatter(grad_joint_bias, "fsdp", scatter_dimension=1, tiled=True),
        lax.psum_scatter(grad_out_weight, "fsdp", scatter_dimension=0, tiled=True),
        lax.psum_scatter(grad_out_bias, "fsdp", scatter_dimension=0, tiled=True),
        lax.psum_scatter(grad_gain_two, "fsdp", scatter_dimension=0, tiled=True),
        lax.psum_scatter(grad_shift_two, "fsdp", scatter_dimension=0, tiled=True),
        lax.psum_scatter(grad_up_weight, "fsdp", scatter_dimension=0, tiled=True),
        lax.psum_scatter(grad_up_bias, "fsdp", scatter_dimension=0, tiled=True),
        lax.psum_scatter(grad_down_weight, "fsdp", scatter_dimension=0, tiled=True),
        lax.psum_scatter(grad_down_bias, "fsdp", scatter_dimension=0, tiled=True),
    )
    attn_sums = every_sum[:6]
    mlp_sums = every_sum[6:]
    totals = (
        lax.psum(attn_sums[0].astype(jnp.bfloat16), "seq").astype(jnp.float32),
        lax.psum(attn_sums[1].astype(jnp.bfloat16), "seq").astype(jnp.float32),
        lax.psum(attn_sums[2].astype(jnp.bfloat16), "seq").astype(jnp.float32),
        lax.psum(attn_sums[3].astype(jnp.bfloat16), "seq").astype(jnp.float32),
        lax.psum(attn_sums[4].astype(jnp.bfloat16), "seq").astype(jnp.float32),
        lax.psum(attn_sums[5].astype(jnp.bfloat16), "seq").astype(jnp.float32),
        lax.psum(mlp_sums[0].astype(jnp.bfloat16), "seq").astype(jnp.float32),
        lax.psum(mlp_sums[1].astype(jnp.bfloat16), "seq").astype(jnp.float32),
        lax.psum(mlp_sums[2].astype(jnp.bfloat16), "seq").astype(jnp.float32),
        lax.psum(mlp_sums[3].astype(jnp.bfloat16), "seq").astype(jnp.float32),
        lax.psum(mlp_sums[4].astype(jnp.bfloat16), "seq").astype(jnp.float32),
        lax.psum(mlp_sums[5].astype(jnp.bfloat16), "seq").astype(jnp.float32),
    )
    return (
        output.astype(jnp.bfloat16)[None],
        grad_inputs[None],
        totals[0],
        totals[1],
        totals[2],
        totals[3],
        totals[4],
        totals[5],
        totals[6],
        totals[7],
        totals[8],
        totals[9],
        totals[10],
        totals[11],
    )


def solution(mesh):
    in_specs = (
        P("fsdp", "seq", None),
        P("fsdp", None),
        P("fsdp"),
        P("fsdp"),
        P("fsdp", None),
        P(None, "fsdp"),
        P("fsdp", None),
        P("fsdp"),
        P("fsdp"),
        P("fsdp"),
        P("fsdp", None),
        P("fsdp"),
        P("fsdp", None),
        P("fsdp"),
        P("fsdp", "seq", None),
    )
    out_specs = (
        P("fsdp", "seq", None),
        P("fsdp", "seq", None),
        P("fsdp"),
        P("fsdp"),
        P("fsdp", None),
        P(None, "fsdp"),
        P("fsdp", None),
        P("fsdp"),
        P("fsdp"),
        P("fsdp"),
        P("fsdp", None),
        P("fsdp"),
        P("fsdp", None),
        P("fsdp"),
    )
    return jax.shard_map(
        per_device, mesh=mesh, in_specs=in_specs, out_specs=out_specs, check_vma=False
    )
```

profile of v0, /device:TPU:0, one launch (start us, length us, event | category | flops | bytes accessed | tf_op | source)
XLA Modules:
  0.0 1121.6 jit_solution(8430259839319301549)
XLA Ops:
  10.1 23.6 %all-gather = bf16[16,64,2]{1,2,0:T(2,128)(2,1)S(1)} all-gather(bf16[1,64,2]{1,2,0:T(2,128)(2,1)} %bitcast.245), channel_id=1, replica_groups=mesh['seq'=2,'fsdp'=16] {'fsdp'}, dimensions={0}, use_global_device_ids=true | all-gather | bytes 4352 | tf_op jit(solution)/shard_map/all_gather | solution.py:102
  38.8 59.6 %all-reduce.14 = (bf16[1024]{0:T(1024)(128)(2,1)S(1)}, bf16[1024]{0:T(1024)(128)(2,1)S(1)}, bf16[1024]{0:T(1024)(128)(2,1)S(1)}, bf16[1024]{0:T(1024)(128)(2,1)}...) all-reduce(bf16[1024]{0:T(1024)(128)(2,1)S(1)} %dynamic-update-slic, ...), channel_id=1, replica_groups=mesh['seq'=2,'fsdp'=16] {'fsdp'}, use_global_device_ids=true, to_apply=%add.1 | all-reduce | flops 6144 | bytes 24576
  98.5 8.1 add_convert_fusion
  106.7 8.3 reshape.247
  115.0 8.6 copy.73
  123.6 5.5 all-to-all-start
  129.2 31.7 %all-to-all-done = bf16[512,3,2,512]{0,3,1,2:T(8,128)(2,1)} async-done(((bf16[512,3,2,512]{0,3,1,2:T(8,128)(2,1)}), bf16[512,3,2,512]{0,3,1,2:T(8,128)(2,1)}, u32[]{:S(2)}, u32[]{:S(2)}) %all-to-all-start) | async-done | bytes 3145760 | tf_op jit(solution)/shard_map/all_to_all | solution.py:114
  160.9 6.8 copy.74
  167.7 6.1 reshape.248
  173.8 3.3 slice_bitcast_fusion
  178.9 1.8 copy.76
  180.6 2.0 copy.77
  182.7 47.9 %while.24 = (s32[]{:T(128)}, bf16[8,1024,64]{1,2,0:T(8,128)(2,1)}, f32[8,1024]{1,0:T(8,128)S(1)}, bf16[8,1024,64]{2,1,0:T(8,128)(2,1)}, bf16[8,1024,64]{2,1,0:T(...) while((s32[]{:T(128)}, bf16[8,1024,64]{1,2,0:T(8,128)(2,1)}, ...), condition=%wide.region_5.6_spmd.clone, body=%wide.region_2.5_spmd.clone.sunk | while | flops 282131456 | bytes 13548157 | solution.py:53
  183.3 3.2 fusion.152
  189.3 3.2 fusion.152
  195.2 3.2 fusion.152
  201.2 3.3 fusion.152
  207.3 3.2 fusion.152
  213.3 3.2 fusion.152
  219.2 3.2 fusion.152
  225.2 3.2 fusion.152
  231.2 3.4 reduce.7
  234.6 2.3 copy.99
  236.9 2.6 reshape.301
  239.5 4.4 all-to-all-start.1
  244.0 19.0 %all-gather.1 = bf16[16,1,256]{2,1,0:T(2,128)(2,1)S(1)} all-gather(bf16[1,1,256]{2,1,0:T(2,128)(2,1)S(1)} %reshape.275), channel_id=1, replica_groups=mesh['seq'=2,'fsdp'=16] {'fsdp'}, dimensions={0}, use_global_device_ids=true | all-gather | bytes 8704 | tf_op jit(solution)/shard_map/all_gather | solution.py:132
  263.0 2.0 reshape.302
  266.2 2.4 copy.79
  268.6 3.3 fusion.115
  272.3 10.6 fusion.109
  282.9 14.3 %convert_reduce_fusion = (f32[4096]{0:T(1024)}, bf16[512,4096]{1,0:T(8,128)(2,1)S(1)}) fusion(f32[512,4096]{1,0:T(8,128)} %fusion.109, f32[4096]{0:T(1024)S(1)} %bitcast.240, bf16[4096,1024]{1,0:T(8,128)(2,1)} %all-gather.13.cloned.1.call-done, bf16[1,512,1024]{2,1,0:T(8,128)(2,1)S(1)} %copy-done.6), kind=kOutput, calls=%fused_computation.72 | convolution fusion | flops 4343197696 | bytes 22052864 | tf_op jit(solution)/shard_map/dot_general | solution.py:32
  297.2 5.0 multiply_reduce_fusion.1
  307.9 3.6 all-to-all-start.2
  311.6 3.3 fusion.116
  315.0 10.9 all-to-all-done.2
  327.9 99.5 %while.25 = (s32[]{:T(128)}, bf16[8,3,1024,64]{2,3,0,1:T(8,128)(2,1)}, bf16[8,1024,64]{2,1,0:T(8,128)(2,1)}, bf16[8,1024,64]{2,1,0:T(8,128)(2,1)}, f32[8]{0:T(12...) while((s32[]{:T(128)}, ...), condition=%wide.region_12.13_spmd.clone, body=%wide.region_10.12_spmd.clone.sunk | while | flops 688323584 | bytes 34241164 | solution.py:71
  330.1 4.3 multiply_reduce_fusion.5
  342.6 4.3 multiply_reduce_fusion.5
  355.0 4.3 multiply_reduce_fusion.5
  367.5 4.3 multiply_reduce_fusion.5
  379.9 4.3 multiply_reduce_fusion.5
  392.3 4.3 multiply_reduce_fusion.5
  404.7 4.3 multiply_reduce_fusion.5
  417.1 4.3 multiply_reduce_fusion.5
  427.3 7.6 copy.87
  434.9 51.4 %all_to_all.60 = bf16[1024,3,1,512]{3,1,2,0:T(4,128)(2,1)S(1)} all-to-all(bf16[1024,3,1,512]{3,1,2,0:T(4,128)(2,1)} %copy.87), channel_id=1, replica_groups=mesh['seq'=2,'fsdp'=16] {'seq'}, dimensions={0} | all-to-all | bytes 6291456 | tf_op jit(solution)/shard_map/all_to_all | solution.py:175
  487.1 2.8 copy.89
  490.0 10.5 fusion.88
  500.8 16.2 %fusion.108 = f32[1024,4096]{1,0:T(8,128)} fusion(bf16[512,4096]{1,0:T(8,128)(2,1)} %copy-done.33, f32[512,1024]{1,0:T(8,128)} %copy-done.4, f32[1024]{0:T(1024)S(1)} %convert_element_type.192, f32[1024]{0:T(1024)S(1)} %convert_element_type.191, f32[512]{0:T(512)S(1)} %fusion.106, f32[512]{0:T(512)S(1)} %broadcast_multiply_fusion), kind=kOutput, calls=%fused_computation.153 | convolution fusion | flops 4297588736 | bytes 23080960 | tf_op jit(solution)/shard_map/dot_general | solution.py:26
  517.1 17.9 %fusion.91 = f32[4096,1024]{1,0:T(8,128)} fusion(bf16[1,512,1024]{2,1,0:T(8,128)(2,1)} %param.33, f32[512,4096]{1,0:T(8,128)} %fusion.109, f32[4096]{0:T(1024)S(1)} %bitcast.241), kind=kOutput, calls=%fused_computation.116 | convolution fusion | flops 4315938816 | bytes 26230784 | tf_op jit(solution)/shard_map/dot_general | solution.py:26
  538.8 12.9 %fusion.85 = bf16[1,512,1024]{2,1,0:T(8,128)(2,1)} fusion(f32[512,1024]{1,0:T(8,128)} %copy-done.4, bf16[4096,1024]{1,0:T(8,128)(2,1)} %all-gather.13.cloned.1.call-done, f32[1024]{0:T(1024)S(1)} %convert_element_type.196, f32[512,4096]{1,0:T(8,128)} %fusion.109, f32[4096]{0:T(1024)S(1)} %bitcast.242), kind=kOutput, calls=%fused_computation.109 | convolution fusion | flops 4317511680 | bytes 19943424 | tf_op jit(solution)/shard_map/dot_general | solution.py:22
  553.4 79.2 %reduce-scatter.8.cloned.1.call-done = f32[64,3072]{1,0:T(8,128)} async-done(((f32[1024,3072]{1,0:T(8,128)}), f32[64,3072]{1,0:T(8,128)}) %reduce-scatter.8.cloned.1.call-update) | async-done | bytes 786448 | tf_op jit(solution)/shard_map/reduce_scatter | solution.py:188
  632.6 1.9 convert_element_type.208
  634.5 178.8 %reduce-scatter.12.cloned.1.call-done = f32[64,4096]{1,0:T(8,128)} async-done(((f32[1024,4096]{1,0:T(8,128)}), f32[64,4096]{1,0:T(8,128)}) %reduce-scatter.12.cloned.1.call-update) | async-done | bytes 1048592 | tf_op jit(solution)/shard_map/reduce_scatter | solution.py:194
  813.4 2.1 convert_element_type.222
  815.4 178.5 %reduce-scatter.14.cloned.1.call-done = f32[256,1024]{1,0:T(8,128)} async-done(((f32[4096,1024]{1,0:T(8,128)}), f32[256,1024]{1,0:T(8,128)}) %reduce-scatter.14.cloned.1.call-update) | async-done | bytes 1048592 | tf_op jit(solution)/shard_map/reduce_scatter | solution.py:196
  993.9 2.1 convert_element_type.227
  996.1 6.9 fusion.110
  1004.8 2.1 convert_reduce_fusion.3
  1007.0 59.6 %all-reduce.13 = (bf16[1024]{0:T(1024)(128)(2,1)S(1)}, bf16[1024]{0:T(1024)(128)(2,1)S(1)}, bf16[1024]{0:T(1024)(128)(2,1)S(1)}, bf16[1024]{0:T(1024)(128)(2,1)S...) all-reduce(f32[1024]{0:T(1024)S(1)} %get-tuple-element.229, ...), channel_id=2, replica_groups=mesh['seq'=2,'fsdp'=16] {'fsdp'}, use_global_device_ids=true, to_apply=%region_16.17.clone | all-reduce | flops 10240 | bytes 61440
  1068.0 5.1 all-reduce.15
  1077.3 30.3 %all-reduce.19.cloned.1.call-done = (bf16[64,3072]{1,0:T(8,128)(2,1)}, bf16[64,1024]{1,0:T(8,128)(2,1)}, bf16[64,4096]{1,0:T(8,128)(2,1)}, bf16[256,1024]{1,0:T(8,128)(2,1)}) async-done(((bf16[64,3072]{1,0:T(8,128)(2,1)}, bf16[64,1024]{1,0:T(8,128)(2,1)}, bf16[64,4096]{1,0:T(8,128)(2,1)}, bf16[256,1024]{1,0:T(8,128)(2,1)}), (bf16[64,3072]{1,0:T(8,128)(2,1)}, bf16[64,1024]{1,0:T(8,128)(2,1)}, ...) | async-done | bytes 1572880 | tf_op jit(solution)/shard_map/psum | solution.py:204
  1107.6 2.0 convert_element_type.209
  1111.2 2.1 convert_element_type.223
  (276 shorter events, 121.5 us)
Async XLA Ops:
  7.2 29.0 %copy-start.23 = (u32[32]{0:T(128)S(1)}, u32[32]{0:T(128)}, u32[]{:S(2)}) copy-start(u32[32]{0:T(128)} %constant.97) | copy-start | bytes 388
  7.2 28.0 %copy-start = (bf16[1,512,1024]{2,1,0:T(8,128)(2,1)S(1)}, bf16[1,512,1024]{2,1,0:T(8,128)(2,1)}, u32[]{:S(2)}) copy-start(bf16[1,512,1024]{2,1,0:T(8,128)(2,1)} %param.19) | copy-start | bytes 3145732
  7.2 30.2 %copy-start.26 = (bf16[64]{0:T(256)(128)(2,1)S(1)}, bf16[64]{0:T(256)(128)(2,1)}, u32[]{:S(2)}) copy-start(bf16[64]{0:T(256)(128)(2,1)} %param.22) | copy-start | bytes 388
  7.2 30.5 %copy-start.27 = (bf16[64]{0:T(256)(128)(2,1)S(1)}, bf16[64]{0:T(256)(128)(2,1)}, u32[]{:S(2)}) copy-start(bf16[64]{0:T(256)(128)(2,1)} %param.21) | copy-start | bytes 388
  7.2 30.7 %copy-start.28 = (bf16[64]{0:T(256)(128)(2,1)S(1)}, bf16[64]{0:T(256)(128)(2,1)}, u32[]{:S(2)}) copy-start(bf16[64]{0:T(256)(128)(2,1)} %param.26) | copy-start | bytes 388
  7.2 30.9 %copy-start.29 = (bf16[64]{0:T(256)(128)(2,1)S(1)}, bf16[64]{0:T(256)(128)(2,1)}, u32[]{:S(2)}) copy-start(bf16[64]{0:T(256)(128)(2,1)} %param.32) | copy-start | bytes 388
  7.2 31.1 %copy-start.30 = (bf16[64]{0:T(256)(128)(2,1)S(1)}, bf16[64]{0:T(256)(128)(2,1)}, u32[]{:S(2)}) copy-start(bf16[64]{0:T(256)(128)(2,1)} %param.28) | copy-start | bytes 388
  7.3 31.4 %copy-start.31 = (bf16[64]{0:T(256)(128)(2,1)S(1)}, bf16[64]{0:T(256)(128)(2,1)}, u32[]{:S(2)}) copy-start(bf16[64]{0:T(256)(128)(2,1)} %param.27) | copy-start | bytes 388
  7.3 91.3 %all-gather.7.cloned.1.call-start = ((), (), s32[]{:S(2)}) async-start(), calls=%async_computation.9 | async-start | bytes 6684672 | tf_op jit(solution)/shard_map/all_gather | solution.py:101
  8.0 260.6 %all-gather.9.cloned.1.call-start = ((), (), s32[]{:S(2)}) async-start(), calls=%async_computation.10 | async-start | bytes 2228224 | tf_op jit(solution)/shard_map/all_gather | solution.py:103
  8.7 263.5 %all-gather.11.cloned.1.call-start = ((), (), s32[]{:S(2)}) async-start(), calls=%async_computation.11 | async-start | bytes 8912896 | tf_op jit(solution)/shard_map/all_gather | solution.py:131
  9.5 273.4 %all-gather.13.cloned.1.call-start = ((), (), s32[]{:S(2)}) async-start(), calls=%async_computation.12 | async-start | bytes 8912896 | tf_op jit(solution)/shard_map/all_gather | solution.py:133
  35.2 71.5 %copy-start.13 = (f32[512]{0:T(512)}, f32[512]{0:T(512)S(1)}, u32[]{:S(2)}) copy-start(f32[512]{0:T(512)S(1)} %broadcast_multiply_fusion.1) | copy-start | bytes 6148
  35.6 0.6 copy-start.17
  35.6 71.1 %copy-start.15 = (f32[512]{0:T(512)}, f32[512]{0:T(512)S(1)}, u32[]{:S(2)}) copy-start(f32[512]{0:T(512)S(1)} %fusion.105) | copy-start | bytes 6148
  98.5 8.2 copy-start.20
  98.5 8.2 copy-start.11
  123.6 37.3 %all-to-all-start = ((bf16[512,3,2,512]{0,3,1,2:T(8,128)(2,1)}), bf16[512,3,2,512]{0,3,1,2:T(8,128)(2,1)}, u32[]{:S(2)}, u32[]{:S(2)}) async-start(bf16[512,3,2,512]{0,3,1,2:T(8,128)(2,1)} %copy.73), calls=%async_computation | async-start | bytes 6291456 | tf_op jit(solution)/shard_map/all_to_all | solution.py:114
  178.9 3.8 copy-start.25
  230.6 8.9 copy-start.5
  234.6 9.4 copy-start.32
  239.5 23.5 %all-to-all-start.1 = ((bf16[2,2,131072]{2,1,0:T(2,128)(2,1)}), bf16[2,2,131072]{2,1,0:T(2,128)(2,1)}, u32[]{:S(2)}, u32[]{:S(2)}) async-start(bf16[2,2,131072]{2,1,0:T(2,128)(2,1)} %reshape.301), calls=%async_computation.1 | async-start | bytes 2097152 | tf_op jit(solution)/shard_map/all_to_all | solution.py:124
  271.8 30.4 %copy-start.4 = (f32[512,1024]{1,0:T(8,128)}, f32[512,1024]{1,0:T(8,128)S(1)}, u32[]{:S(2)}) copy-start(f32[512,1024]{1,0:T(8,128)S(1)} %get-tuple-element.313) | copy-start | bytes 6291460
  272.2 10.7 copy-start.6
  282.9 14.3 %copy-start.24 = (bf16[1024,4096]{1,0:T(8,128)(2,1)S(1)}, bf16[1024,4096]{1,0:T(8,128)(2,1)}, u32[]{:S(2)}) copy-start(bf16[1024,4096]{1,0:T(8,128)(2,1)} %all-gather.11.cloned.1.call-done) | copy-start | bytes 25165828
  297.2 5.0 copy-start.33
  302.9 1.3 copy-start.2
  302.9 2.4 copy-start.9
  306.6 5.0 copy-start.8
  307.9 17.9 %all-to-all-start.2 = ((bf16[512,2,512]{0,2,1:T(8,128)(2,1)}), bf16[512,2,512]{0,2,1:T(8,128)(2,1)S(1)}, u32[]{:S(2)}, u32[]{:S(2)}) async-start(bf16[512,2,512]{0,2,1:T(8,128)(2,1)} %bitcast.19), calls=%async_computation.2 | async-start | bytes 2097152 | tf_op jit(solution)/shard_map/all_to_all | solution.py:171
  311.5 240.2 %reduce-scatter.10.cloned.1.call-start = ((), (), s32[]{:S(2)}) async-start(), calls=%async_computation.14 | async-start | bytes 4456448 | tf_op jit(solution)/shard_map/reduce_scatter | solution.py:190
  314.9 317.7 %reduce-scatter.8.cloned.1.call-start = ((), (), s32[]{:S(2)}) async-start(), calls=%async_computation.13 | async-start | bytes 13369344 | tf_op jit(solution)/shard_map/reduce_scatter | solution.py:188
  487.1 2.9 copy-start.12
  487.1 2.9 copy-start.14
  487.1 2.9 copy-start.16
  487.1 2.9 copy-start.21
  500.5 312.8 %reduce-scatter.12.cloned.1.call-start = ((), (), s32[]{:S(2)}) async-start(), calls=%async_computation.15 | async-start | bytes 17825792 | tf_op jit(solution)/shard_map/reduce_scatter | solution.py:194
  517.0 476.9 %reduce-scatter.14.cloned.1.call-start = ((), (), s32[]{:S(2)}) async-start(), calls=%async_computation.16 | async-start | bytes 17825792 | tf_op jit(solution)/shard_map/reduce_scatter | solution.py:196
  535.0 0.7 copy-start.22
  535.0 532.1 %reduce-scatter.16.cloned.1.call-start = ((), (), s32[]{:S(2)}) async-start(), calls=%async_computation.17 | async-start | bytes 557056
  538.5 569.1 %all-reduce.19.cloned.1.call-start = ((), (), s32[]{:S(2)}) async-start(), calls=%async_computation.18 | async-start | bytes 3145728 | tf_op jit(solution)/shard_map/psum | solution.py:204
  551.7 444.4 %copy-start.1 = (bf16[1,512,1024]{2,1,0:T(8,128)(2,1)S(1)}, bf16[1,512,1024]{2,1,0:T(8,128)(2,1)}, u32[]{:S(2)}) copy-start(bf16[1,512,1024]{2,1,0:T(8,128)(2,1)} %param.19) | copy-start | bytes 3145732
  996.1 6.9 copy-start.18
  1003.0 1.6 copy-start.3
  1003.0 1.9 copy-start.7
  1004.8 2.1 copy-start.19
  1107.6 5.7 copy-start.10
Sparse Core Ops, SparseCore 0:
  10.4 64.7 all-gather.6
  77.3 40.1 all-gather.8
  119.6 72.9 all-gather.10
  194.7 72.9 all-gather.12
  315.8 70.6 reduce-scatter.9
  500.7 131.9 reduce-scatter.7
  636.7 176.6 reduce-scatter.11
  817.5 176.4 reduce-scatter.13
  998.1 55.2 reduce-scatter.15
  1056.8 50.7 all-reduce.18
where the time goes:
time: 1130 us; the launch traced here: 1120 us
  waiting for transfers between devices  512 us (45%)
  matrix products  227 us (20%)
  blocking collectives  218 us (19%)
  local copies, waits for them, and re-layouts  82.9 us (7%)
  other arithmetic  49.6 us (4%)
  between operations  17.2 us (2%)
  starting transfers between devices  14.4 us (1%)
    reduce_scatter x1, waiting for transfers between devices, per_device(): lax.psum_scatter(grad_up_weight, 'fsdp', scatter_dimension=0, tiled=True)  179 us
    reduce_scatter x1, waiting for transfers between devices, per_device(): lax.psum_scatter(grad_down_weight, 'fsdp', scatter_dimension=0, tiled=True)  178 us
    unnamed x2, blocking collectives  119 us
    dot_general x28, matrix products, right_contract(): lax.dot_general(left, right, (((1,), (1,)), ((), ())), preferred_element_...  100 us
    reduce_scatter x1, waiting for transfers between devices, per_device(): lax.psum_scatter(grad_joint_weight, 'fsdp', scatter_dimension=0, tiled=True)  79.2 us
    dot_general x20, matrix products, left_contract(): lax.dot_general(left, right, (((0,), (0,)), ((), ())), preferred_element_...  67.8 us
    dot_general x20, matrix products, matmul(): return jnp.dot(left, right, preferred_element_type=jnp.float32)  58.5 us
    all_to_all x1, blocking collectives, per_device(): lax.all_to_all(grad_stack, 'seq', split_axis=0, concat_axis=2, tiled=True)  51.4 us
  transfers between devices with their start and end apart: 13, of which 6 were waited for; matrix products, arithmetic and copies ran while one was open for 29% of the time, Pallas kernels for 0%

commit v1 on v0

--- a/solution.py
+++ b/solution.py
@@ -6,6 +6,10 @@
 HEADS = 16
 HEAD_DIM = 64
 EPSILON = 1e-05
+
+
+def deliver_core(mine):
+    return lax.all_gather(mine, axis_name="seq").sum(axis=0)
 
 
 def scaled_norm(values, gain):
@@ -201,7 +205,7 @@
     totals = (
         lax.psum(attn_sums[0].astype(jnp.bfloat16), "seq").astype(jnp.float32),
         lax.psum(attn_sums[1].astype(jnp.bfloat16), "seq").astype(jnp.float32),
-        lax.psum(attn_sums[2].astype(jnp.bfloat16), "seq").astype(jnp.float32),
+        deliver_core(attn_sums[2].astype(jnp.bfloat16)).astype(jnp.float32),
         lax.psum(attn_sums[3].astype(jnp.bfloat16), "seq").astype(jnp.float32),
         lax.psum(attn_sums[4].astype(jnp.bfloat16), "seq").astype(jnp.float32),
         lax.psum(attn_sums[5].astype(jnp.bfloat16), "seq").astype(jnp.float32),

time: 1130 us -> 1010 us (0.89)
  waiting for transfers between devices: 512 us -> 377 us
  blocking collectives: 218 us -> 233 us
    reduce_scatter x1, waiting for transfers between devices: 179 us -> 0.01 us  [per_device(): lax.psum_scatter(grad_up_weight, 'fsdp', scatter_dimension=0, tiled=True)]
    reduce_scatter x1, waiting for transfers between devices: 79.2 us -> 121 us  [per_device(): lax.psum_scatter(grad_joint_weight, 'fsdp', scatter_dimension=0, tiled=True)]
    all_gather x0 -> x1, blocking collectives: none -> 14.6 us  [deliver_core(): return lax.all_gather(mine, axis_name='seq').sum(axis=0)]
    unnamed x103 -> x111, local copies, waits for them, and re-layouts: 22.1 us -> 23.4 us
  transfers between devices with their start and end apart: 13 -> 13, of which waited for: 6 -> 5; matrix products, arithmetic and copies ran while one was open for 29% -> 32% of each run, Pallas kernels for 0% -> 0%
where the time goes in v1:
time: 1010 us; the launch traced here: 999 us
  waiting for transfers between devices  377 us (37%)
  blocking collectives  233 us (23%)
  matrix products  222 us (22%)
  local copies, waits for them, and re-layouts  84.9 us (8%)
  other arithmetic  50.7 us (5%)
  between operations  17.2 us (2%)
  starting transfers between devices  14.6 us (1%)
    reduce_scatter x1, waiting for transfers between devices, per_device(): lax.psum_scatter(grad_down_weight, 'fsdp', scatter_dimension=0, tiled=True)  177 us
    reduce_scatter x1, waiting for transfers between devices, per_device(): lax.psum_scatter(grad_joint_weight, 'fsdp', scatter_dimension=0, tiled=True)  121 us
    unnamed x2, blocking collectives  119 us
    dot_general x28, matrix products, right_contract(): lax.dot_general(left, right, (((1,), (1,)), ((), ())), preferred_element_...  103 us
    dot_general x20, matrix products, left_contract(): lax.dot_general(left, right, (((0,), (0,)), ((), ())), preferred_element_...  60.8 us
    dot_general x20, matrix products, matmul(): return jnp.dot(left, right, preferred_element_type=jnp.float32)  58.2 us
    all_to_all x1, blocking collectives, per_device(): lax.all_to_all(grad_stack, 'seq', split_axis=0, concat_axis=2, tiled=True)  51.3 us
    all_to_all x1, waiting for transfers between devices, per_device(): lax.all_to_all(joint, 'seq', split_axis=2, concat_axis=0, tiled=True)  31.7 us
  transfers between devices with their start and end apart: 13, of which 5 were waited for; matrix products, arithmetic and copies ran while one was open for 32% of the time, Pallas kernels for 0%

profile of v1, /device:TPU:0, one launch (start us, length us, event | category | flops | bytes accessed | tf_op | source)
XLA Modules:
  0.0 999.4 jit_solution(13422148159150170370)
XLA Ops:
  10.1 23.6 %all-gather.1 = bf16[16,64,2]{1,2,0:T(2,128)(2,1)S(1)} all-gather(bf16[1,64,2]{1,2,0:T(2,128)(2,1)} %bitcast.247), channel_id=1, replica_groups=mesh['seq'=2,'fsdp'=16] {'fsdp'}, dimensions={0}, use_global_device_ids=true | all-gather | bytes 4352 | tf_op jit(solution)/shard_map/all_gather | solution.py:106
  38.8 59.6 %all-reduce.14 = (bf16[1024]{0:T(1024)(128)(2,1)S(1)}, bf16[1024]{0:T(1024)(128)(2,1)S(1)}, bf16[1024]{0:T(1024)(128)(2,1)S(1)}, bf16[1024]{0:T(1024)(128)(2,1)}...) all-reduce(bf16[1024]{0:T(1024)(128)(2,1)S(1)} %dynamic-update-slic, ...), channel_id=1, replica_groups=mesh['seq'=2,'fsdp'=16] {'fsdp'}, use_global_device_ids=true, to_apply=%add.1 | all-reduce | flops 6144 | bytes 24576
  98.5 8.1 add_convert_fusion
  106.7 8.3 reshape.247
  115.0 8.6 copy.73
  123.6 5.5 all-to-all-start
  129.2 31.7 %all-to-all-done = bf16[512,3,2,512]{0,3,1,2:T(8,128)(2,1)} async-done(((bf16[512,3,2,512]{0,3,1,2:T(8,128)(2,1)}), bf16[512,3,2,512]{0,3,1,2:T(8,128)(2,1)}, u32[]{:S(2)}, u32[]{:S(2)}) %all-to-all-start) | async-done | bytes 3145760 | tf_op jit(solution)/shard_map/all_to_all | solution.py:118
  160.9 6.8 copy.74
  167.7 6.1 reshape.248
  173.8 3.3 slice_bitcast_fusion
  180.7 2.0 copy.77
  182.7 47.9 %while.24 = (s32[]{:T(128)}, bf16[8,1024,64]{1,2,0:T(8,128)(2,1)}, f32[8,1024]{1,0:T(8,128)S(1)}, bf16[8,1024,64]{2,1,0:T(8,128)(2,1)}, bf16[8,1024,64]{2,1,0:T(...) while((s32[]{:T(128)}, bf16[8,1024,64]{1,2,0:T(8,128)(2,1)}, ...), condition=%wide.region_5.6_spmd.clone, body=%wide.region_2.5_spmd.clone.sunk | while | flops 282131456 | bytes 13548157 | solution.py:57
  183.3 3.2 fusion.152
  189.3 3.2 fusion.152
  195.3 3.2 fusion.152
  201.2 3.3 fusion.152
  207.3 3.2 fusion.152
  213.3 3.2 fusion.152
  219.3 3.2 fusion.152
  225.2 3.2 fusion.152
  231.2 3.4 reduce.8
  234.6 2.3 copy.100
  236.8 2.6 reshape.302
  239.5 4.4 all-to-all-start.1
  244.0 19.0 %all-gather.2 = bf16[16,1,256]{2,1,0:T(2,128)(2,1)S(1)} all-gather(bf16[1,1,256]{2,1,0:T(2,128)(2,1)S(1)} %reshape.276), channel_id=1, replica_groups=mesh['seq'=2,'fsdp'=16] {'fsdp'}, dimensions={0}, use_global_device_ids=true | all-gather | bytes 8704 | tf_op jit(solution)/shard_map/all_gather | solution.py:136
  266.3 2.3 copy.79
  268.6 3.3 fusion.115
  272.3 10.6 %fusion.109 = f32[512,4096]{1,0:T(8,128)} fusion(bf16[1024,4096]{1,0:T(8,128)(2,1)} %all-gather.12.cloned.1.call-done, f32[512,1024]{1,0:T(8,128)S(1)} %get-tuple-element.312, f32[1024]{0:T(1024)S(1)} %convert_element_type.194, f32[1024]{0:T(1024)S(1)} %convert_element_type.193, f32[512]{0:T(512)S(1)} %fusion.106, f32[512]{0:T(512)S(1)} %broadcast_multiply_fusion), kind=kOutput, calls=%fused_computation.154 | convolution fusion | flops 4297588736 | bytes 18886656 | tf_op jit(solution)/shard_map/dot_general | solution.py:26
  283.0 14.3 %convert_reduce_fusion = (f32[4096]{0:T(1024)}, bf16[512,4096]{1,0:T(8,128)(2,1)S(1)}) fusion(f32[512,4096]{1,0:T(8,128)} %fusion.109, f32[4096]{0:T(1024)S(1)} %bitcast.242, bf16[4096,1024]{1,0:T(8,128)(2,1)} %all-gather.14.cloned.1.call-done, bf16[1,512,1024]{2,1,0:T(8,128)(2,1)S(1)} %copy-done.8), kind=kOutput, calls=%fused_computation.72 | convolution fusion | flops 4343197696 | bytes 22052864 | tf_op jit(solution)/shard_map/dot_general | solution.py:36
  297.3 5.0 multiply_reduce_fusion.1
  305.6 3.3 fusion.116
  309.0 11.0 %fusion.108 = f32[1024,4096]{1,0:T(8,128)} fusion(bf16[512,4096]{1,0:T(8,128)(2,1)} %copy-done.37, f32[512,1024]{1,0:T(8,128)S(1)} %get-tuple-element.312, f32[1024]{0:T(1024)S(1)} %convert_element_type.194, f32[1024]{0:T(1024)S(1)} %convert_element_type.193, f32[512]{0:T(512)S(1)} %fusion.106, f32[512]{0:T(512)S(1)} %broadcast_multiply_fusion), kind=kOutput, calls=%fused_computation.153 | convolution fusion | flops 4297588736 | bytes 23080960 | tf_op jit(solution)/shard_map/dot_general | solution.py:30
  320.2 16.1 %fusion.91 = f32[4096,1024]{1,0:T(8,128)} fusion(bf16[1,512,1024]{2,1,0:T(8,128)(2,1)S(1)} %copy-done.8, f32[512,4096]{1,0:T(8,128)} %fusion.109, f32[4096]{0:T(1024)S(1)} %bitcast.243), kind=kOutput, calls=%fused_computation.116 | convolution fusion | flops 4315938816 | bytes 26230784 | tf_op jit(solution)/shard_map/dot_general | solution.py:30
  338.3 2.3 convolution_convert_fusion
  340.6 2.3 copy.90
  342.8 3.6 all-to-all-start.2
  346.7 14.1 %all-to-all-done.2 = bf16[512,2,512]{0,2,1:T(8,128)(2,1)S(1)} async-done(((bf16[512,2,512]{0,2,1:T(8,128)(2,1)}), bf16[512,2,512]{0,2,1:T(8,128)(2,1)S(1)}, u32[]{:S(2)}, u32[]{:S(2)}) %all-to-all-start.2) | async-done | bytes 1048608 | tf_op jit(solution)/shard_map/all_to_all | solution.py:175
  362.6 99.9 %while.25 = (s32[]{:T(128)}, bf16[8,3,1024,64]{2,3,0,1:T(8,128)(2,1)}, bf16[8,1024,64]{2,1,0:T(8,128)(2,1)}, bf16[8,1024,64]{2,1,0:T(8,128)(2,1)}, f32[8]{0:T(12...) while((s32[]{:T(128)}, ...), condition=%wide.region_12.13_spmd.clone, body=%wide.region_10.12_spmd.clone.sunk | while | flops 688323584 | bytes 34241164 | solution.py:75
  364.9 4.3 multiply_reduce_fusion.5
  377.3 4.3 multiply_reduce_fusion.5
  389.8 4.4 multiply_reduce_fusion.5
  402.5 4.3 multiply_reduce_fusion.5
  415.0 4.3 multiply_reduce_fusion.5
  427.4 4.3 multiply_reduce_fusion.5
  439.8 4.3 multiply_reduce_fusion.5
  452.3 4.3 multiply_reduce_fusion.5
  462.5 7.6 copy.87
  470.1 51.3 %all_to_all.60 = bf16[1024,3,1,512]{3,1,2,0:T(4,128)(2,1)S(1)} all-to-all(bf16[1024,3,1,512]{3,1,2,0:T(4,128)(2,1)} %copy.87), channel_id=1, replica_groups=mesh['seq'=2,'fsdp'=16] {'seq'}, dimensions={0} | all-to-all | bytes 6291456 | tf_op jit(solution)/shard_map/all_to_all | solution.py:179
  522.2 2.8 copy.89
  526.7 10.5 %fusion.88 = f32[1024,3072]{1,0:T(8,128)} fusion(bf16[512,3072]{0,1:T(8,128)(2,1)} %bitcast.233, bf16[1,512,1024]{2,1,0:T(8,128)(2,1)} %param.19, f32[1024]{0:T(1024)S(1)} %copy-done.25, f32[1024]{0:T(1024)S(1)} %copy-done.16, f32[512]{0:T(512)S(1)} %copy-done.20, f32[512]{0:T(512)S(1)} %copy-done.18), kind=kOutput, calls=%fused_computation.112 | convolution fusion | flops 3224371200 | bytes 16789504 | tf_op jit(solution)/shard_map/dot_general | solution.py:30
  539.2 12.5 %fusion.85 = bf16[1,512,1024]{2,1,0:T(8,128)(2,1)} fusion(f32[512,1024]{1,0:T(8,128)S(1)} %copy-done.5, bf16[4096,1024]{1,0:T(8,128)(2,1)} %all-gather.14.cloned.1.call-done, f32[1024]{0:T(1024)S(1)} %convert_element_type.198, f32[512,4096]{1,0:T(8,128)} %fusion.109, f32[4096]{0:T(1024)S(1)} %bitcast.244), kind=kOutput, calls=%fused_computation.109 | convolution fusion | flops 4317511680 | bytes 19943424 | tf_op jit(solution)/shard_map/dot_general | solution.py:26
  551.8 7.9 fusion.110
  561.3 2.1 convert_element_type.224
  563.4 177.4 %reduce-scatter.14.cloned.1.call-done = f32[256,1024]{1,0:T(8,128)} async-done(((f32[4096,1024]{1,0:T(8,128)}), f32[256,1024]{1,0:T(8,128)}) %reduce-scatter.14.cloned.1.call-update) | async-done | bytes 1048592 | tf_op jit(solution)/shard_map/reduce_scatter | solution.py:200
  740.8 2.1 convert_element_type.229
  743.0 2.7 fusion.77
  745.7 2.2 convert_reduce_fusion.3
  747.9 59.6 %all-reduce.13 = (bf16[1024]{0:T(1024)(128)(2,1)S(1)}, bf16[1024]{0:T(1024)(128)(2,1)S(1)}, bf16[1024]{0:T(1024)(128)(2,1)S(1)}, bf16[1024]{0:T(1024)(128)(2,1)S...) all-reduce(f32[1024]{0:T(1024)S(1)} %get-tuple-element.229, ...), channel_id=3, replica_groups=mesh['seq'=2,'fsdp'=16] {'fsdp'}, use_global_device_ids=true, to_apply=%region_16.17.clone | all-reduce | flops 10240 | bytes 61440
  808.8 4.9 all-reduce.15
  817.9 120.5 %reduce-scatter.8.cloned.1.call-done = f32[64,3072]{1,0:T(8,128)} async-done(((f32[1024,3072]{1,0:T(8,128)}), f32[64,3072]{1,0:T(8,128)}) %reduce-scatter.8.cloned.1.call-update) | async-done | bytes 786448 | tf_op jit(solution)/shard_map/reduce_scatter | solution.py:192
  939.7 14.6 %all-gather = bf16[128,3072]{1,0:T(8,128)(2,1)S(1)} all-gather(bf16[64,3072]{1,0:T(8,128)(2,1)S(1)} %convert_element_type.210), channel_id=2, replica_groups=mesh['seq'=2,'fsdp'=16] {'seq'}, dimensions={0}, use_global_device_ids=true | all-gather | bytes 1179648 | tf_op jit(solution)/shard_map/all_gather | solution.py:12
  955.5 30.8 %all-reduce.19.cloned.1.call-done = (bf16[64,1024]{1,0:T(8,128)(2,1)}, bf16[64,4096]{1,0:T(8,128)(2,1)}, bf16[256,1024]{1,0:T(8,128)(2,1)}) async-done(((bf16[64,1024]{1,0:T(8,128)(2,1)}, bf16[64,4096]{1,0:T(8,128)(2,1)}, bf16[256,1024]{1,0:T(8,128)(2,1)}), (bf16[64,1024]{1,0:T(8,128)(2,1)}, bf16[64,4096]{1,0:T(8,128)(2,1)}, bf16[256,1024]{1,0:T(8,128)(2,1)})) %all-reduce.19.cloned.1.call-update) | async-done | bytes 1179664 | tf_op jit(solution)/shard_map/psum | solution.py:210
  987.9 2.1 convert_element_type.225
  990.0 2.1 convert_element_type.230
  (286 shorter events, 124.4 us)
Async XLA Ops:
  7.2 29.0 %copy-start.27 = (u32[32]{0:T(128)S(1)}, u32[32]{0:T(128)}, u32[]{:S(2)}) copy-start(u32[32]{0:T(128)} %constant.98) | copy-start | bytes 388
  7.2 28.0 %copy-start = (bf16[1,512,1024]{2,1,0:T(8,128)(2,1)S(1)}, bf16[1,512,1024]{2,1,0:T(8,128)(2,1)}, u32[]{:S(2)}) copy-start(bf16[1,512,1024]{2,1,0:T(8,128)(2,1)} %param.19) | copy-start | bytes 3145732
  7.2 30.2 %copy-start.30 = (bf16[64]{0:T(256)(128)(2,1)S(1)}, bf16[64]{0:T(256)(128)(2,1)}, u32[]{:S(2)}) copy-start(bf16[64]{0:T(256)(128)(2,1)} %param.22) | copy-start | bytes 388
  7.2 30.5 %copy-start.31 = (bf16[64]{0:T(256)(128)(2,1)S(1)}, bf16[64]{0:T(256)(128)(2,1)}, u32[]{:S(2)}) copy-start(bf16[64]{0:T(256)(128)(2,1)} %param.21) | copy-start | bytes 388
  7.2 30.7 %copy-start.32 = (bf16[64]{0:T(256)(128)(2,1)S(1)}, bf16[64]{0:T(256)(128)(2,1)}, u32[]{:S(2)}) copy-start(bf16[64]{0:T(256)(128)(2,1)} %param.26) | copy-start | bytes 388
  7.2 30.9 %copy-start.33 = (bf16[64]{0:T(256)(128)(2,1)S(1)}, bf16[64]{0:T(256)(128)(2,1)}, u32[]{:S(2)}) copy-start(bf16[64]{0:T(256)(128)(2,1)} %param.32) | copy-start | bytes 388
  7.2 31.1 %copy-start.34 = (bf16[64]{0:T(256)(128)(2,1)S(1)}, bf16[64]{0:T(256)(128)(2,1)}, u32[]{:S(2)}) copy-start(bf16[64]{0:T(256)(128)(2,1)} %param.28) | copy-start | bytes 388
  7.3 31.4 %copy-start.35 = (bf16[64]{0:T(256)(128)(2,1)S(1)}, bf16[64]{0:T(256)(128)(2,1)}, u32[]{:S(2)}) copy-start(bf16[64]{0:T(256)(128)(2,1)} %param.27) | copy-start | bytes 388
  7.3 91.3 %all-gather.8.cloned.1.call-start = ((), (), s32[]{:S(2)}) async-start(), calls=%async_computation.9 | async-start | bytes 6684672 | tf_op jit(solution)/shard_map/all_gather | solution.py:105
  8.0 260.6 %all-gather.10.cloned.1.call-start = ((), (), s32[]{:S(2)}) async-start(), calls=%async_computation.10 | async-start | bytes 2228224 | tf_op jit(solution)/shard_map/all_gather | solution.py:107
  8.7 263.6 %all-gather.12.cloned.1.call-start = ((), (), s32[]{:S(2)}) async-start(), calls=%async_computation.11 | async-start | bytes 8912896 | tf_op jit(solution)/shard_map/all_gather | solution.py:135
  9.5 273.5 %all-gather.14.cloned.1.call-start = ((), (), s32[]{:S(2)}) async-start(), calls=%async_computation.12 | async-start | bytes 8912896 | tf_op jit(solution)/shard_map/all_gather | solution.py:137
  35.2 71.5 %copy-start.17 = (f32[512]{0:T(512)}, f32[512]{0:T(512)S(1)}, u32[]{:S(2)}) copy-start(f32[512]{0:T(512)S(1)} %broadcast_multiply_fusion.1) | copy-start | bytes 6148
  35.6 0.6 copy-start.21
  35.6 71.1 %copy-start.19 = (f32[512]{0:T(512)}, f32[512]{0:T(512)S(1)}, u32[]{:S(2)}) copy-start(f32[512]{0:T(512)S(1)} %fusion.105) | copy-start | bytes 6148
  98.5 8.2 copy-start.24
  98.5 8.2 copy-start.15
  123.6 37.3 %all-to-all-start = ((bf16[512,3,2,512]{0,3,1,2:T(8,128)(2,1)}), bf16[512,3,2,512]{0,3,1,2:T(8,128)(2,1)}, u32[]{:S(2)}, u32[]{:S(2)}) async-start(bf16[512,3,2,512]{0,3,1,2:T(8,128)(2,1)} %copy.73), calls=%async_computation | async-start | bytes 6291456 | tf_op jit(solution)/shard_map/all_to_all | solution.py:118
  178.9 3.8 copy-start.29
  230.6 8.9 copy-start.6
  234.6 9.5 copy-start.36
  239.5 23.6 %all-to-all-start.1 = ((bf16[2,2,131072]{2,1,0:T(2,128)(2,1)}), bf16[2,2,131072]{2,1,0:T(2,128)(2,1)}, u32[]{:S(2)}, u32[]{:S(2)}) async-start(bf16[2,2,131072]{2,1,0:T(2,128)(2,1)} %reshape.302), calls=%async_computation.1 | async-start | bytes 2097152 | tf_op jit(solution)/shard_map/all_to_all | solution.py:128
  243.9 315.8 %reduce-scatter.10.cloned.1.call-start = ((), (), s32[]{:S(2)}) async-start(), calls=%async_computation.14 | async-start | bytes 4456448 | tf_op jit(solution)/shard_map/reduce_scatter | solution.py:194
  271.9 37.1 %copy-start.4 = (f32[512,1024]{1,0:T(8,128)}, f32[512,1024]{1,0:T(8,128)S(1)}, u32[]{:S(2)}) copy-start(f32[512,1024]{1,0:T(8,128)S(1)} %get-tuple-element.312) | copy-start | bytes 6291460
  272.3 10.7 %copy-start.8 = (bf16[1,512,1024]{2,1,0:T(8,128)(2,1)S(1)}, bf16[1,512,1024]{2,1,0:T(8,128)(2,1)}, u32[]{:S(2)}) copy-start(bf16[1,512,1024]{2,1,0:T(8,128)(2,1)} %param.33) | copy-start | bytes 3145732
  283.0 14.3 %copy-start.28 = (bf16[1024,4096]{1,0:T(8,128)(2,1)S(1)}, bf16[1024,4096]{1,0:T(8,128)(2,1)}, u32[]{:S(2)}) copy-start(bf16[1024,4096]{1,0:T(8,128)(2,1)} %all-gather.12.cloned.1.call-done) | copy-start | bytes 25165828
  297.3 5.0 copy-start.37
  303.0 1.3 copy-start.2
  303.0 2.7 copy-start.10
  304.7 1.0 copy-start.13
  309.0 252.4 %reduce-scatter.12.cloned.1.call-start = ((), (), s32[]{:S(2)}) async-start(), calls=%async_computation.15 | async-start | bytes 17825792 | tf_op jit(solution)/shard_map/reduce_scatter | solution.py:198
  320.0 420.8 %reduce-scatter.14.cloned.1.call-start = ((), (), s32[]{:S(2)}) async-start(), calls=%async_computation.16 | async-start | bytes 17825792 | tf_op jit(solution)/shard_map/reduce_scatter | solution.py:200
  336.3 1.7 copy-start.12
  336.3 2.0 copy-start.14
  342.8 17.9 %all-to-all-start.2 = ((bf16[512,2,512]{0,2,1:T(8,128)(2,1)}), bf16[512,2,512]{0,2,1:T(8,128)(2,1)S(1)}, u32[]{:S(2)}, u32[]{:S(2)}) async-start(bf16[512,2,512]{0,2,1:T(8,128)(2,1)} %bitcast.19), calls=%async_computation.2 | async-start | bytes 2097152 | tf_op jit(solution)/shard_map/all_to_all | solution.py:175
  346.4 461.6 %reduce-scatter.16.cloned.1.call-start = ((), (), s32[]{:S(2)}) async-start(), calls=%async_computation.17 | async-start | bytes 557056
  525.0 1.6 copy-start.16
  525.0 1.6 copy-start.18
  525.0 1.6 copy-start.20
  525.0 1.6 copy-start.25
  526.6 411.9 %reduce-scatter.8.cloned.1.call-start = ((), (), s32[]{:S(2)}) async-start(), calls=%async_computation.13 | async-start | bytes 13369344 | tf_op jit(solution)/shard_map/reduce_scatter | solution.py:192
  537.2 0.7 copy-start.26
  537.2 2.0 copy-start.5
  537.2 449.1 %all-reduce.19.cloned.1.call-start = ((), (), s32[]{:S(2)}) async-start(), calls=%async_computation.18 | async-start | bytes 2359296 | tf_op jit(solution)/shard_map/psum | solution.py:210
  539.2 12.6 %copy-start.1 = (bf16[1,512,1024]{2,1,0:T(8,128)(2,1)S(1)}, bf16[1,512,1024]{2,1,0:T(8,128)(2,1)}, u32[]{:S(2)}) copy-start(bf16[1,512,1024]{2,1,0:T(8,128)(2,1)} %param.19) | copy-start | bytes 3145732
  539.2 12.6 %copy-start.11 = (bf16[512,3,2,1,512]{0,4,2,1,3:T(8,128)(2,1)S(1)}, bf16[512,3,2,1,512]{0,4,2,1,3:T(8,128)(2,1)}, u32[]{:S(2)}) copy-start(bf16[512,3,2,1,512]{0,4,2,1,3:T(8,128)(2,1)} %copy.89) | copy-start | bytes 9437188
  551.8 7.9 copy-start.22
  563.4 182.3 %copy-start.3 = (f32[512,1024]{1,0:T(8,128)S(1)}, f32[512,1024]{1,0:T(8,128)}, u32[]{:S(2)}) copy-start(f32[512,1024]{1,0:T(8,128)} %copy-done.2) | copy-start | bytes 6291460
  742.9 2.7 copy-start.7
  743.0 2.7 copy-start.9
  745.7 2.2 copy-start.23
Sparse Core Ops, SparseCore 0:
  10.4 64.7 all-gather.7
  77.3 40.1 all-gather.9
  119.6 72.9 all-gather.11
  194.7 72.9 all-gather.13
  309.1 70.6 reduce-scatter.9
  383.8 176.4 reduce-scatter.11
  564.4 176.4 reduce-scatter.13
  745.0 55.2 reduce-scatter.15
  804.3 134.0 reduce-scatter.7
  941.9 44.3 all-reduce.18
